TPU v7x, 256 devices: a whole 4x4x8 slice. The times are simulated.
256 devices in a mesh: tm: 16 (over z, core), height: 4 (over x), chan: 4 (over y).
Axes of the slice: x: 4, y: 4, z: 8, core: 2. Of those that a mesh axis runs over, the one named last changes fastest.
Arguments:
- frames: bfloat16 [32, 16, 256, 128], P('tm', 'height', 'chan'), may hold values from -6 to 6
- grad_out: bfloat16 [32, 16, 256, 128], P('tm', 'height', 'chan'), may hold values from -6 to 6
- weight_one: bfloat16 [256, 3, 3, 3, 256], P('chan'), may hold values from -0.078125 to 0.078125
- weight_two: bfloat16 [256, 3, 3, 3, 256], P('chan'), may hold values from -0.078125 to 0.078125
Outputs:
- grad_frames: bfloat16 [32, 16, 256, 128], P('tm', 'height', 'chan')
- grad_one: float32 [256, 3, 3, 3, 256], P('chan')
- grad_two: float32 [256, 3, 3, 3, 256], P('chan')
All inputs are finite; a program needn't handle non-finite values.
Results may differ from a plain program's by a relative error of at most 0.015.
Values may be sent and summed in bfloat16 or wider, within the bound.
No kernel may reach another device: no remote copies, remote signals or barrier semaphores. Data moves between devices by JAX's collectives and lax.ppermute only.
A program may use at most 128 MiB of HBM per device.

v0:
```python
import jax
import jax.numpy as jnp
from jax import lax
from jax.sharding import PartitionSpec as P


def passed_along(block, axis, distance):
    devices = range(lax.axis_size(axis))
    route = [(i - distance, i) for i in devices if i - distance in devices]
    return lax.ppermute(block, axis, route)


def extended(cells, sides, width):
    for axis, dim in sides:
        count = lax.axis_size(axis)
        ends = count - 1
        head = lax.slice_in_dim(cells, 0, width, axis=dim)
        tail = lax.slice_in_dim(cells, cells.shape[dim] - width, cells.shape[dim], axis=dim)
        cells = jnp.concatenate(
            [
                lax.ppermute(tail, axis, [(i, (i + 1) % count) for i in range(ends)]),
                cells,
                lax.ppermute(head, axis, [((i + 1) % count, i) for i in range(ends)]),
            ],
            axis=dim,
        )
    return cells


def product(form, left, right):
    return jnp.einsum(form, left, right, preferred_element_type=jnp.float32)


def shift_cols(block, offset):
    if offset == 0:
        return block
    edge = jnp.zeros(block.shape[:3] + (1,), block.dtype)
    if offset > 0:
        return jnp.concatenate([block[..., 1:], edge], 3)
    return jnp.concatenate([edge, block[..., :-1]], 3)


def forward_taps(padded, weight):
    frame_count = padded.shape[0] - 2
    row_count = padded.shape[1] - 2
    col_count = padded.shape[3]
    summed = jnp.zeros((frame_count, row_count, weight.shape[0], col_count), jnp.float32)
    for col_tap in range(3):
        partial_sum = jnp.zeros((frame_count, row_count, weight.shape[0], col_count), jnp.float32)
        for time_tap in range(3):
            for row_tap in range(3):
                window = padded[time_tap : time_tap + frame_count, row_tap : row_tap + row_count]
                partial_sum = partial_sum + product(
                    "frcw,oc->frow", window, weight[:, time_tap, row_tap, col_tap, :]
                )
        summed = summed + shift_cols(partial_sum, col_tap - 1)
    return summed


def backward_taps(padded, weight):
    frame_count = padded.shape[0] - 2
    row_count = padded.shape[1] - 2
    col_count = padded.shape[3]
    summed = jnp.zeros((frame_count, row_count, weight.shape[4], col_count), jnp.float32)
    for col_tap in range(3):
        partial_sum = jnp.zeros((frame_count, row_count, weight.shape[4], col_count), jnp.float32)
        for time_tap in range(3):
            for row_tap in range(3):
                window = padded[
                    2 - time_tap : 2 - time_tap + frame_count, 2 - row_tap : 2 - row_tap + row_count
                ]
                partial_sum = partial_sum + product(
                    "frow,oc->frcw", window, weight[:, time_tap, row_tap, col_tap, :]
                )
        summed = summed + shift_cols(partial_sum, 1 - col_tap)
    return summed


def forward_filter(padded, gradient):
    frame_count, row_count, out_width, col_count = gradient.shape
    moved = [shift_cols(gradient, 1 - col_tap) for col_tap in range(3)]
    pieces = []
    for time_tap in range(3):
        for row_tap in range(3):
            window = padded[time_tap : time_tap + frame_count, row_tap : row_tap + row_count]
            for col_tap in range(3):
                pieces.append(product("frcw,frow->oc", window, moved[col_tap]))
    return jnp.stack(pieces, 1).reshape(out_width, 3, 3, 3, padded.shape[2])


def backward_filter(source, padded):
    frame_count, row_count, in_width, col_count = source.shape
    moved = [shift_cols(padded, 1 - col_tap) for col_tap in range(3)]
    pieces = []
    for time_tap in range(3):
        for row_tap in range(3):
            for col_tap in range(3):
                window = moved[col_tap][
                    2 - time_tap : 2 - time_tap + frame_count, 2 - row_tap : 2 - row_tap + row_count
                ]
                pieces.append(product("frcw,frow->oc", source, window))
    return jnp.stack(pieces, 1).reshape(padded.shape[2], 3, 3, 3, in_width)


def on_device(frames, grad_out, weight_one, weight_two):
    earlier = passed_along(frames, "tm", 1)
    frames_time = jnp.concatenate([earlier, frames], 0)
    frames_rows = extended(frames_time, (("height", 1),), 1)
    frames_panel = lax.all_gather(frames_rows, "chan", axis=2, tiled=True)
    pre = forward_taps(frames_panel, weight_one)
    act = jax.nn.silu(pre).astype(jnp.bfloat16)
    later = passed_along(grad_out, "tm", -1)
    grads_time = jnp.concatenate([grad_out, later], 0)
    grads_padded = extended(grads_time, (("height", 1),), 1)
    act_full = lax.all_gather(act, "chan", axis=2, tiled=True)
    part_two = backward_filter(act_full, grads_padded)
    sigmoid_pre = jax.nn.sigmoid(pre)
    grad_act = lax.psum_scatter(
        backward_taps(grads_padded, weight_two), "chan", scatter_dimension=2, tiled=True
    )
    grad_pre = (grad_act * sigmoid_pre * (1.0 + pre * (1.0 - sigmoid_pre))).astype(jnp.bfloat16)
    pre_later = passed_along(grad_pre, "tm", -1)
    pre_time = jnp.concatenate([grad_pre, pre_later], 0)
    pre_padded = extended(pre_time, (("height", 1),), 1)
    grad_frames = lax.psum_scatter(
        backward_taps(pre_padded, weight_one).astype(jnp.bfloat16),
        "chan",
        scatter_dimension=2,
        tiled=True,
    )
    part_one = forward_filter(frames_panel, grad_pre)
    grad_one, grad_two = lax.psum((part_one, part_two), ("tm", "height"))
    return (grad_frames, grad_one, grad_two)


def solution(mesh):
    in_specs = (
        P("tm", "height", "chan", None),
        P("tm", "height", "chan", None),
        P("chan", None, None, None, None),
        P("chan", None, None, None, None),
    )
    out_specs = (
        P("tm", "height", "chan", None),
        P("chan", None, None, None, None),
        P("chan", None, None, None, None),
    )
    return jax.shard_map(
        on_device, mesh=mesh, in_specs=in_specs, out_specs=out_specs, check_vma=False
    )
```

profile of v0, /device:TPU:8, one launch (start us, length us, event | category | flops | bytes accessed | tf_op | source)
XLA Modules:
  0.0 437.9 jit_solution(17015021139338158347)
XLA Ops:
  7.2 1.4 collective-permute-start
  8.7 1.3 convolution_bitcast_fusion.21
  9.9 1.3 convolution_bitcast_fusion.25
  11.2 0.3 convolution_bitcast_fusion.23
  12.7 3.4 collective-permute-start.2
  16.1 1.3 collective-permute-start.1
  17.4 0.3 convolution_bitcast_fusion.26
  17.7 0.3 convolution_bitcast_fusion.22
  18.1 0.3 convolution_bitcast_fusion.24
  19.8 2.5 collective-permute-done.1
  22.6 0.3 convolution_bitcast_fusion.15
  22.9 0.3 convolution_bitcast_fusion.16
  23.2 0.3 convolution_bitcast_fusion.18
  23.6 0.3 convolution_bitcast_fusion.2
  23.9 0.3 convolution_bitcast_fusion.4
  24.2 1.1 fusion.1
  25.3 1.1 fusion.10
  26.4 1.2 slice_add_fusion
  27.6 1.1 convolution_bitcast_fusion.11
  28.7 1.1 convolution_bitcast_fusion.12
  29.8 1.1 convolution_bitcast_fusion.8
  30.9 1.1 convolution_bitcast_fusion.9
  32.0 1.1 convolution_bitcast_fusion.7
  33.1 1.6 fusion.36
  34.6 1.3 copy.128
  36.0 3.0 collective-permute-start.3
  39.1 1.0 collective-permute-done.3
  40.1 3.4 collective-permute-start.4
  43.5 1.3 collective-permute-start.5
  44.8 0.6 collective-permute-done.4
  45.4 4.3 collective-permute-done.5
  49.7 0.8 pad_maximum_fusion
  50.7 0.6 dynamic-slice
  52.2 37.8 %all-reduce.17.cloned.1.call-done = f32[2,4,256,128]{3,1,0,2:T(4,128)} async-done(((f32[2,4,256,128]{3,1,0,2:T(4,128)}), f32[2,4,256,128]{3,1,0,2:T(4,128)}) %all-reduce.17.cloned.1.call-update) | async-done | bytes 1048592
  90.0 1.7 constant_dynamic-slice_fusion.1
  91.7 30.6 %all-gather.2.cloned.1.call-done = bf16[4,6,256,128]{3,2,1,0:T(8,128)(2,1)} async-done(((bf16[4,6,64,128]{3,2,1,0:T(8,128)(2,1)}), bf16[4,6,256,128]{3,2,1,0:T(8,128)(2,1)}) %all-gather.2.cloned.1.call-update) | async-done | bytes 1572880 | tf_op jit(solution)/shard_map/all_gather | solution.py:109
  122.3 1.4 fusion.148
  123.7 1.3 convolution_add_fusion.13
  125.1 1.0 convolution_add_fusion.12
  126.1 1.0 convolution_add_fusion.11
  132.7 1.3 collective-permute-start.6
  135.1 13.3 %all_gather.7 = bf16[2,4,256,128]{3,1,0,2:T(4,128)(2,1)S(1)} all-gather(bf16[2,4,64,128]{3,1,0,2:T(4,128)(2,1)S(1)} %copy.131), channel_id=1, replica_groups=mesh['tm'=16,'height'=4,'chan'=4] {'chan'}, dimensions={2}, use_global_device_ids=true | all-gather | bytes 655360 | tf_op jit(solution)/shard_map/all_gather | solution.py:115
  163.1 3.4 collective-permute-start.8
  166.5 1.5 collective-permute-start.7
  170.7 2.0 collective-permute-done.7
  173.3 0.6 fusion.33
  173.9 0.3 fusion.27
  175.3 0.3 fusion.193
  175.6 0.3 fusion.228
  176.3 0.3 fusion.220
  176.6 0.3 fusion.217
  177.0 0.6 fusion.17
  177.9 0.6 fusion.26
  178.4 0.4 fusion.37
  178.8 1.1 copy.130
  180.0 0.9 fusion.72
  180.9 0.9 fusion.71
  181.8 0.9 fusion.70
  182.8 45.5 %all-reduce.19.cloned.1.call-done = bf16[2,4,256,128]{3,1,0,2:T(4,128)(2,1)} async-done(((bf16[2,4,256,128]{3,1,0,2:T(4,128)(2,1)}), bf16[2,4,256,128]{3,1,0,2:T(4,128)(2,1)}) %all-reduce.19.cloned.1.call-update) | async-done | bytes 524304
  228.3 0.9 constant_dynamic-slice_fusion
  229.2 0.7 copy.159
  229.9 197.3 %all-reduce.21.cloned.1.call-done = (f32[64,3,3,3,256]{4,0,3,2,1:T(8,128)}, f32[64,3,3,3,256]{4,0,3,2,1:T(8,128)}) async-done(((f32[64,3,3,3,256]{4,0,3,2,1:T(8,128)}, f32[64,3,3,3,256]{4,0,3,2,1:T(8,128)}), (f32[64,3,3,3,256]{4,0,3,2,1:T(8,128)}, f32[64,3,3,3,256]{4,0,3,2,1:T(8,128)})) %all-reduce.21.cloned.1.call-update) | async-done | bytes 3538960 | tf_op jit(solution)/shard_map/psum | solution.py:132
  427.2 3.0 copy.391
  430.2 1.2 copy.392
  (145 shorter events, 29.5 us)
Async XLA Ops:
  7.2 4.1 copy-start.2
  7.2 4.1 copy-start.6
  7.2 82.9 %all-reduce.17.cloned.1.call-start = ((), (), s32[]{:S(2)}) async-start(), calls=%async_computation.1 | async-start | bytes 2097152
  7.2 4.4 collective-permute-start
  12.7 5.8 %collective-permute-start.2 = (bf16[4,1,64,128]{3,2,1,0:T(8,128)(2,1)S(1)}, bf16[4,1,64,128]{3,2,1,0:T(8,128)(2,1)S(1)}, u32[]{:S(2)}, u32[]{:S(2)}) collective-permute-start(bf16[4,1,64,128]{3,2,1,0:T(8,128)(2,1)S(1)} %get-tuple-element.20), channel_id=1, source_target_pairs={{0,4},{4,8},{8,12},{1,5},{5,9},{9,13},{2,6},{6,10},{10,14},{3,7},{... | collective-permute-start | bytes 196616 | tf_op jit(solution)/shard_map/ppermute | solution.py:21
  16.1 6.2 %collective-permute-start.1 = (bf16[4,1,64,128]{3,2,1,0:T(8,128)(2,1)S(1)}, bf16[4,1,64,128]{3,2,1,0:T(8,128)(2,1)S(1)}, u32[]{:S(2)}, u32[]{:S(2)}) collective-permute-start(bf16[4,1,64,128]{3,2,1,0:T(8,128)(2,1)S(1)} %get-tuple-element.19), channel_id=1, source_target_pairs={{4,0},{8,4},{12,8},{5,1},{9,5},{13,9},{6,2},{10,6},{14,10},{7,3},{... | collective-permute-start | bytes 196616 | tf_op jit(solution)/shard_map/ppermute | solution.py:23
  34.6 1.4 copy-start.8
  36.0 14.8 %copy-start.9 = (u32[256]{0:T(256)S(1)}, u32[256]{0:T(256)}, u32[]{:S(2)}) copy-start(u32[256]{0:T(256)} %constant.34) | copy-start | bytes 3076
  36.0 86.3 %all-gather.2.cloned.1.call-start = ((), (), s32[]{:S(2)}) async-start(), calls=%async_computation | async-start | bytes 1966080 | tf_op jit(solution)/shard_map/all_gather | solution.py:109
  36.0 4.0 collective-permute-start.3
  40.1 5.3 %collective-permute-start.4 = (bf16[4,1,64,128]{3,2,1,0:T(8,128)(2,1)S(1)}, bf16[4,1,64,128]{3,2,1,0:T(8,128)(2,1)S(1)}, u32[]{:S(2)}, u32[]{:S(2)}) collective-permute-start(bf16[4,1,64,128]{3,2,1,0:T(8,128)(2,1)S(1)} %get-tuple-element.17), channel_id=1, source_target_pairs={{0,4},{4,8},{8,12},{1,5},{5,9},{9,13},{2,6},{6,10},{10,14},{3,7},{... | collective-permute-start | bytes 196616 | tf_op jit(solution)/shard_map/ppermute | solution.py:21
  43.5 6.2 %collective-permute-start.5 = (bf16[4,1,64,128]{3,2,1,0:T(8,128)(2,1)S(1)}, bf16[4,1,64,128]{3,2,1,0:T(8,128)(2,1)S(1)}, u32[]{:S(2)}, u32[]{:S(2)}) collective-permute-start(bf16[4,1,64,128]{3,2,1,0:T(8,128)(2,1)S(1)} %get-tuple-element.18), channel_id=1, source_target_pairs={{4,0},{8,4},{12,8},{5,1},{9,5},{13,9},{6,2},{10,6},{14,10},{7,3},{... | collective-permute-start | bytes 196616 | tf_op jit(solution)/shard_map/ppermute | solution.py:23
  50.5 177.8 %all-reduce.19.cloned.1.call-start = ((), (), s32[]{:S(2)}) async-start(), calls=%async_computation.2 | async-start | bytes 1048576
  122.3 2.8 copy-start
  123.7 3.3 copy-start.1
  131.3 1.0 copy-start.7
  132.7 30.3 %collective-permute-start.6 = (bf16[2,4,64,128]{3,2,1,0:T(8,128)(2,1)S(1)}, bf16[2,4,64,128]{3,2,1,0:T(8,128)(2,1)S(1)}, u32[]{:S(2)}, u32[]{:S(2)}) collective-permute-start(bf16[2,4,64,128]{3,2,1,0:T(8,128)(2,1)S(1)} %get-tuple-element.14), channel_id=1, source_target_pairs={{16,0},{32,16},{48,32},{64,48},{80,64},{96,80},{112,96},{128,112},... | collective-permute-start | bytes 393224 | tf_op jit(solution)/shard_map/ppermute | solution.py:10
  156.1 1.4 copy-start.3
  163.0 6.0 %copy-start.5 = (f32[64,27,256]{2,0,1:T(8,128)}, f32[64,27,256]{2,0,1:T(8,128)S(1)}, u32[]{:S(2)}) copy-start(f32[64,27,256]{2,0,1:T(8,128)S(1)} %fusion.73) | copy-start | bytes 5308420
  163.1 6.9 %collective-permute-start.8 = (bf16[4,1,64,128]{3,2,1,0:T(8,128)(2,1)S(1)}, bf16[4,1,64,128]{3,2,1,0:T(8,128)(2,1)S(1)}, u32[]{:S(2)}, u32[]{:S(2)}) collective-permute-start(bf16[4,1,64,128]{3,2,1,0:T(8,128)(2,1)S(1)} %get-tuple-element.15), channel_id=1, source_target_pairs={{0,4},{4,8},{8,12},{1,5},{5,9},{9,13},{2,6},{6,10},{10,14},{3,7},{... | collective-permute-start | bytes 196616 | tf_op jit(solution)/shard_map/ppermute | solution.py:21
  166.5 6.2 %collective-permute-start.7 = (bf16[4,1,64,128]{3,2,1,0:T(8,128)(2,1)S(1)}, bf16[4,1,64,128]{3,2,1,0:T(8,128)(2,1)S(1)}, u32[]{:S(2)}, u32[]{:S(2)}) collective-permute-start(bf16[4,1,64,128]{3,2,1,0:T(8,128)(2,1)S(1)} %get-tuple-element.16), channel_id=1, source_target_pairs={{4,0},{8,4},{12,8},{5,1},{9,5},{13,9},{6,2},{10,6},{14,10},{7,3},{... | collective-permute-start | bytes 196616 | tf_op jit(solution)/shard_map/ppermute | solution.py:23
  179.9 247.2 %all-reduce.21.cloned.1.call-start = ((), (), s32[]{:S(2)}) async-start(), calls=%async_computation.3 | async-start | bytes 7077888 | tf_op jit(solution)/shard_map/psum | solution.py:132
  427.2 3.0 copy-start.4
Sparse Core Ops, SparseCore 0:
  36.1 53.8 all-reduce.16
  92.6 29.7 all-gather.1
  180.1 48.1 all-reduce.18
  232.6 194.5 all-reduce.20
where the time goes:
time: 439 us; the launch traced here: 438 us
  waiting for transfers between devices  322 us (73%)
  matrix products  53.8 us (12%)
  starting transfers between devices  20.4 us (5%)
  between operations  15.3 us (3%)
  blocking collectives  13.3 us (3%)
  local copies, waits for them, and re-layouts  11.5 us (3%)
    psum x1, waiting for transfers between devices, on_device(): grad_one, grad_two = lax.psum((part_one, part_two), ('tm', 'height'))  197 us
    unnamed x6, waiting for transfers between devices  83.4 us
    dot_general x135, matrix products, product(): return jnp.einsum(form, left, right, preferred_element_type=jnp.float32)  53.8 us
    all_gather x1, waiting for transfers between devices, on_device(): frames_panel = lax.all_gather(frames_rows, 'chan', axis=2, tiled=True)  30.6 us
    all_gather x1, blocking collectives, on_device(): act_full = lax.all_gather(act, 'chan', axis=2, tiled=True)  13.3 us
    ppermute x3, starting transfers between devices, extended(): lax.ppermute(tail, axis, [(i, (i + 1) % count) for i in range(ends)])  10.2 us
  transfers between devices with their start and end apart: 13, of which 9 were waited for; matrix products, arithmetic and copies ran while one was open for 7% of the time, Pallas kernels for 0%

commit v1 on v0

--- a/solution.py
+++ b/solution.py
@@ -2,6 +2,11 @@
 import jax.numpy as jnp
 from jax import lax
 from jax.sharding import PartitionSpec as P
+
+
+def exchange_gather(x, axis, along):
+    sent = jnp.stack([x] * lax.axis_size(axis))
+    return jnp.concatenate(lax.all_to_all(sent, axis, 0, 0), axis=along)
 
 
 def passed_along(block, axis, distance):
@@ -112,7 +117,7 @@
     later = passed_along(grad_out, "tm", -1)
     grads_time = jnp.concatenate([grad_out, later], 0)
     grads_padded = extended(grads_time, (("height", 1),), 1)
-    act_full = lax.all_gather(act, "chan", axis=2, tiled=True)
+    act_full = exchange_gather(act, "chan", 2)
     part_two = backward_filter(act_full, grads_padded)
     sigmoid_pre = jax.nn.sigmoid(pre)
     grad_act = lax.psum_scatter(

time: 439 us -> 424 us (0.966)
  blocking collectives: 13.3 us -> 0 us
  waiting for transfers between devices: 322 us -> 316 us
  starting transfers between devices: 20.4 us -> 26 us
  matrix products: 53.8 us -> 48.8 us
    all_gather x1 -> x0, blocking collectives: 13.3 us -> none  [on_device(): act_full = lax.all_gather(act, 'chan', axis=2, tiled=True)]
    unnamed x6, waiting for transfers between devices: 83.4 us -> 76.6 us
    all_to_all x0 -> x1, starting transfers between devices: none -> 5.7 us  [exchange_gather(): return jnp.concatenate(lax.all_to_all(sent, axis, 0, 0), axis=along)]
    dot_general x135, matrix products: 53.8 us -> 48.8 us  [product(): return jnp.einsum(form, left, right, preferred_element_type=jnp.float32)]
    unnamed x28 -> x34, local copies, waits for them, and re-layouts: 8.45 us -> 10.4 us
  transfers between devices with their start and end apart: 13 -> 14, of which waited for: 9 -> 9; matrix products, arithmetic and copies ran while one was open for 7% -> 10% of each run, Pallas kernels for 0% -> 0%
where the time goes in v1:
time: 424 us; the launch traced here: 423 us
  waiting for transfers between devices  316 us (75%)
  matrix products  48.8 us (12%)
  starting transfers between devices  26 us (6%)
  local copies, waits for them, and re-layouts  15.4 us (4%)
  between operations  15.3 us (4%)
    psum x1, waiting for transfers between devices, on_device(): grad_one, grad_two = lax.psum((part_one, part_two), ('tm', 'height'))  197 us
    unnamed x6, waiting for transfers between devices  76.6 us
    dot_general x135, matrix products, product(): return jnp.einsum(form, left, right, preferred_element_type=jnp.float32)  48.8 us
    all_gather x1, waiting for transfers between devices, on_device(): frames_panel = lax.all_gather(frames_rows, 'chan', axis=2, tiled=True)  31.3 us
    unnamed x34, local copies, waits for them, and re-layouts  10.4 us
    ppermute x3, starting transfers between devices, extended(): lax.ppermute(tail, axis, [(i, (i + 1) % count) for i in range(ends)])  10.2 us
    ppermute x3, waiting for transfers between devices, extended(): lax.ppermute(head, axis, [((i + 1) % count, i) for i in range(ends)])  8.97 us
  transfers between devices with their start and end apart: 14, of which 9 were waited for; matrix products, arithmetic and copies ran while one was open for 10% of the time, Pallas kernels for 0%

profile of v1, /device:TPU:8, one launch (start us, length us, event | category | flops | bytes accessed | tf_op | source)
XLA Modules:
  0.0 423.1 jit_solution(4822273328120684125)
XLA Ops:
  7.2 1.4 collective-permute-start
  8.7 1.3 convolution_bitcast_fusion.21
  9.9 1.3 convolution_bitcast_fusion.25
  11.2 0.3 convolution_bitcast_fusion.23
  12.7 3.4 collective-permute-start.2
  16.1 1.3 collective-permute-start.1
  17.4 0.3 convolution_bitcast_fusion.26
  17.7 0.3 convolution_bitcast_fusion.22
  18.1 0.3 convolution_bitcast_fusion.24
  19.8 2.5 collective-permute-done.1
  22.6 0.3 convolution_bitcast_fusion.15
  22.9 0.3 convolution_bitcast_fusion.16
  23.2 0.3 convolution_bitcast_fusion.18
  23.6 0.3 convolution_bitcast_fusion.2
  23.9 0.3 convolution_bitcast_fusion.4
  24.9 1.2 slice_add_fusion
  26.1 0.3 convolution_bitcast_fusion.11
  26.5 0.3 convolution_bitcast_fusion.12
  26.8 0.3 convolution_bitcast_fusion.8
  27.1 0.3 convolution_bitcast_fusion.9
  27.5 0.3 convolution_bitcast_fusion.7
  27.8 0.7 fusion.36
  28.5 1.3 copy.102
  29.9 3.0 collective-permute-start.3
  32.9 1.0 collective-permute-done.3
  34.0 3.4 collective-permute-start.4
  37.4 1.5 collective-permute-start.5
  38.8 0.4 collective-permute-done.4
  39.3 4.3 %collective-permute-done.5 = bf16[4,1,64,128]{3,2,1,0:T(8,128)(2,1)S(1)} collective-permute-done((bf16[4,1,64,128]{3,2,1,0:T(8,128)(2,1)S(1)}, bf16[4,1,64,128]{3,2,1,0:T(8,128)(2,1)S(1)}, u32[]{:S(2)}, u32[]{:S(2)}) %collective-permute-start.5) | collective-permute-done | bytes 65568 | tf_op jit(solution)/shard_map/ppermute | solution.py:28
  43.5 0.8 pad_maximum_fusion
  44.4 0.6 dynamic-slice
  45.9 38.0 %all-reduce.17.cloned.1.call-done = f32[2,4,256,128]{3,1,0,2:T(4,128)} async-done(((f32[2,4,256,128]{3,1,0,2:T(4,128)}), f32[2,4,256,128]{3,1,0,2:T(4,128)}) %all-reduce.17.cloned.1.call-update) | async-done | bytes 1048592
  83.9 1.0 constant_dynamic-slice_fusion.1
  84.9 31.3 %all-gather.2.cloned.1.call-done = bf16[4,6,256,128]{3,2,1,0:T(8,128)(2,1)} async-done(((bf16[4,6,64,128]{3,2,1,0:T(8,128)(2,1)}), bf16[4,6,256,128]{3,2,1,0:T(8,128)(2,1)}) %all-gather.2.cloned.1.call-update) | async-done | bytes 1572880 | tf_op jit(solution)/shard_map/all_gather | solution.py:114
  116.2 1.4 fusion.148
  117.6 1.3 convolution_add_fusion.13
  119.0 1.0 convolution_add_fusion.12
  119.9 1.0 convolution_add_fusion.11
  126.2 1.3 collective-permute-start.6
  127.5 1.3 fusion.238
  128.8 1.3 fusion.190
  130.1 1.3 fusion.214
  131.4 0.9 stack.203
  132.3 5.7 %all-to-all-start = ((bf16[4,2,4,64,128]{4,3,2,1,0:T(8,128)(2,1)}), bf16[4,2,4,64,128]{4,3,2,1,0:T(8,128)(2,1)}, u32[]{:S(2)}, u32[]{:S(2)}) async-start(bf16[4,2,4,64,128]{4,3,2,1,0:T(8,128)(2,1)} %stack.203), calls=%async_computation | async-start | bytes 1048576 | tf_op jit(solution)/shard_map/all_to_all | solution.py:9
  145.8 3.4 collective-permute-start.8
  149.2 1.5 collective-permute-start.7
  152.1 0.3 fusion.231
  153.4 2.2 collective-permute-done.7
  158.3 0.3 fusion.220
  159.2 0.6 fusion.33
  160.1 0.9 copy-done.2
  161.0 0.6 fusion.17
  161.6 0.7 copy-done.1
  162.2 0.6 fusion.26
  163.2 0.4 fusion.37
  163.6 1.1 copy.104
  164.8 1.1 copy.105
  173.7 1.2 copy-done.7
  174.9 38.5 %all-reduce.19.cloned.1.call-done = bf16[2,4,256,128]{3,1,0,2:T(4,128)(2,1)} async-done(((bf16[2,4,256,128]{3,1,0,2:T(4,128)(2,1)}), bf16[2,4,256,128]{3,1,0,2:T(4,128)(2,1)}) %all-reduce.19.cloned.1.call-update) | async-done | bytes 524304
  213.4 0.9 constant_dynamic-slice_fusion
  214.4 0.7 copy.106
  215.0 197.3 %all-reduce.21.cloned.1.call-done = (f32[64,3,3,3,256]{4,0,3,2,1:T(8,128)}, f32[64,3,3,3,256]{4,0,3,2,1:T(8,128)}) async-done(((f32[64,3,3,3,256]{4,0,3,2,1:T(8,128)}, f32[64,3,3,3,256]{4,0,3,2,1:T(8,128)}), (f32[64,3,3,3,256]{4,0,3,2,1:T(8,128)}, f32[64,3,3,3,256]{4,0,3,2,1:T(8,128)})) %all-reduce.21.cloned.1.call-update) | async-done | bytes 3538960 | tf_op jit(solution)/shard_map/psum | solution.py:137
  412.3 3.0 copy.284
  415.3 1.2 copy.285
  (153 shorter events, 30.6 us)
Async XLA Ops:
  7.2 4.1 copy-start.6
  7.2 4.1 copy-start.10
  7.2 76.7 %all-reduce.17.cloned.1.call-start = ((), (), s32[]{:S(2)}) async-start(), calls=%async_computation.2 | async-start | bytes 2097152
  7.2 4.4 %collective-permute-start = (bf16[2,4,64,128]{3,2,1,0:T(8,128)(2,1)}, bf16[2,4,64,128]{3,2,1,0:T(8,128)(2,1)S(1)}, u32[]{:S(2)}, u32[]{:S(2)}) collective-permute-start(bf16[2,4,64,128]{3,2,1,0:T(8,128)(2,1)} %param.5), channel_id=1, source_target_pairs={{16,0},{32,16},{48,32},{64,48},{80,64},{96,80},{112,96},{128,112},... | collective-permute-start | bytes 393224 | tf_op jit(solution)/shard_map/ppermute | solution.py:15
  12.7 5.8 %collective-permute-start.2 = (bf16[4,1,64,128]{3,2,1,0:T(8,128)(2,1)S(1)}, bf16[4,1,64,128]{3,2,1,0:T(8,128)(2,1)S(1)}, u32[]{:S(2)}, u32[]{:S(2)}) collective-permute-start(bf16[4,1,64,128]{3,2,1,0:T(8,128)(2,1)S(1)} %get-tuple-element.20), channel_id=1, source_target_pairs={{0,4},{4,8},{8,12},{1,5},{5,9},{9,13},{2,6},{6,10},{10,14},{3,7},{... | collective-permute-start | bytes 196616 | tf_op jit(solution)/shard_map/ppermute | solution.py:26
  16.1 6.2 %collective-permute-start.1 = (bf16[4,1,64,128]{3,2,1,0:T(8,128)(2,1)S(1)}, bf16[4,1,64,128]{3,2,1,0:T(8,128)(2,1)S(1)}, u32[]{:S(2)}, u32[]{:S(2)}) collective-permute-start(bf16[4,1,64,128]{3,2,1,0:T(8,128)(2,1)S(1)} %get-tuple-element.19), channel_id=1, source_target_pairs={{4,0},{8,4},{12,8},{5,1},{9,5},{13,9},{6,2},{10,6},{14,10},{7,3},{... | collective-permute-start | bytes 196616 | tf_op jit(solution)/shard_map/ppermute | solution.py:28
  28.5 1.4 copy-start.11
  29.8 14.5 %copy-start.12 = (u32[256]{0:T(256)S(1)}, u32[256]{0:T(256)}, u32[]{:S(2)}) copy-start(u32[256]{0:T(256)} %constant.34) | copy-start | bytes 3076
  29.9 86.3 %all-gather.2.cloned.1.call-start = ((), (), s32[]{:S(2)}) async-start(), calls=%async_computation.1 | async-start | bytes 1966080 | tf_op jit(solution)/shard_map/all_gather | solution.py:114
  29.9 4.0 collective-permute-start.3
  34.0 5.3 %collective-permute-start.4 = (bf16[4,1,64,128]{3,2,1,0:T(8,128)(2,1)S(1)}, bf16[4,1,64,128]{3,2,1,0:T(8,128)(2,1)S(1)}, u32[]{:S(2)}, u32[]{:S(2)}) collective-permute-start(bf16[4,1,64,128]{3,2,1,0:T(8,128)(2,1)S(1)} %get-tuple-element.17), channel_id=1, source_target_pairs={{0,4},{4,8},{8,12},{1,5},{5,9},{9,13},{2,6},{6,10},{10,14},{3,7},{... | collective-permute-start | bytes 196616 | tf_op jit(solution)/shard_map/ppermute | solution.py:26
  37.4 6.2 %collective-permute-start.5 = (bf16[4,1,64,128]{3,2,1,0:T(8,128)(2,1)S(1)}, bf16[4,1,64,128]{3,2,1,0:T(8,128)(2,1)S(1)}, u32[]{:S(2)}, u32[]{:S(2)}) collective-permute-start(bf16[4,1,64,128]{3,2,1,0:T(8,128)(2,1)S(1)} %get-tuple-element.18), channel_id=1, source_target_pairs={{4,0},{8,4},{12,8},{5,1},{9,5},{13,9},{6,2},{10,6},{14,10},{7,3},{... | collective-permute-start | bytes 196616 | tf_op jit(solution)/shard_map/ppermute | solution.py:28
  116.2 2.8 copy-start
  117.6 3.3 copy-start.4
  126.2 19.6 %collective-permute-start.6 = (bf16[2,4,64,128]{3,2,1,0:T(8,128)(2,1)S(1)}, bf16[2,4,64,128]{3,2,1,0:T(8,128)(2,1)S(1)}, u32[]{:S(2)}, u32[]{:S(2)}) collective-permute-start(bf16[2,4,64,128]{3,2,1,0:T(8,128)(2,1)S(1)} %get-tuple-element.14), channel_id=1, source_target_pairs={{16,0},{32,16},{48,32},{64,48},{80,64},{96,80},{112,96},{128,112},... | collective-permute-start | bytes 393224 | tf_op jit(solution)/shard_map/ppermute | solution.py:15
  132.3 32.5 %all-to-all-start = ((bf16[4,2,4,64,128]{4,3,2,1,0:T(8,128)(2,1)}), bf16[4,2,4,64,128]{4,3,2,1,0:T(8,128)(2,1)}, u32[]{:S(2)}, u32[]{:S(2)}) async-start(bf16[4,2,4,64,128]{4,3,2,1,0:T(8,128)(2,1)} %stack.203), calls=%async_computation | async-start | bytes 1048576 | tf_op jit(solution)/shard_map/all_to_all | solution.py:9
  138.0 75.4 %all-reduce.19.cloned.1.call-start = ((), (), s32[]{:S(2)}) async-start(), calls=%async_computation.3 | async-start | bytes 1048576
  144.6 6.1 %copy-start.5 = (bf16[64,3,3,3,256]{4,0,3,2,1:T(8,128)(2,1)S(1)}, bf16[64,3,3,3,256]{4,0,3,2,1:T(8,128)(2,1)}, u32[]{:S(2)}) copy-start(bf16[64,3,3,3,256]{4,0,3,2,1:T(8,128)(2,1)} %param.6) | copy-start | bytes 2654212
  145.8 6.0 %copy-start.9 = (f32[64,27,256]{2,0,1:T(8,128)}, f32[64,27,256]{2,0,1:T(8,128)S(1)}, u32[]{:S(2)}) copy-start(f32[64,27,256]{2,0,1:T(8,128)S(1)} %fusion.70) | copy-start | bytes 5308420
  145.8 6.9 %collective-permute-start.8 = (bf16[4,1,64,128]{3,2,1,0:T(8,128)(2,1)S(1)}, bf16[4,1,64,128]{3,2,1,0:T(8,128)(2,1)S(1)}, u32[]{:S(2)}, u32[]{:S(2)}) collective-permute-start(bf16[4,1,64,128]{3,2,1,0:T(8,128)(2,1)S(1)} %get-tuple-element.15), channel_id=1, source_target_pairs={{0,4},{4,8},{8,12},{1,5},{5,9},{9,13},{2,6},{6,10},{10,14},{3,7},{... | collective-permute-start | bytes 196616 | tf_op jit(solution)/shard_map/ppermute | solution.py:26
  149.2 6.5 %collective-permute-start.7 = (bf16[4,1,64,128]{3,2,1,0:T(8,128)(2,1)S(1)}, bf16[4,1,64,128]{3,2,1,0:T(8,128)(2,1)S(1)}, u32[]{:S(2)}, u32[]{:S(2)}) collective-permute-start(bf16[4,1,64,128]{3,2,1,0:T(8,128)(2,1)S(1)} %get-tuple-element.16), channel_id=1, source_target_pairs={{4,0},{8,4},{12,8},{5,1},{9,5},{13,9},{6,2},{10,6},{14,10},{7,3},{... | collective-permute-start | bytes 196616 | tf_op jit(solution)/shard_map/ppermute | solution.py:28
  158.0 1.2 copy-start.3
  159.8 1.2 copy-start.2
  161.0 1.2 copy-start.1
  164.8 247.5 %all-reduce.21.cloned.1.call-start = ((), (), s32[]{:S(2)}) async-start(), calls=%async_computation.4 | async-start | bytes 7077888 | tf_op jit(solution)/shard_map/psum | solution.py:137
  173.6 1.2 copy-start.7
  412.3 3.0 copy-start.8
Sparse Core Ops, SparseCore 0:
  30.0 53.8 all-reduce.16
  86.4 29.7 all-gather.1
  164.9 48.4 all-reduce.18
  217.8 194.5 all-reduce.20
